TPU v7x, 256 devices: a whole 4x4x8 slice. The times are simulated.
256 devices in a mesh: row: 16 (over z_lo, x, core), col: 16 (over y, z_hi).
Axes of the slice: x: 4, y: 4, z: 8 (z_hi: 4, z_lo: 2; z = z_hi * 2 + z_lo), core: 2. Of those that a mesh axis runs over, the one named last changes fastest.
Arguments:
- matrix_tiles: float32 [1, 16, 1, 16, 1024, 1024], P(None, 'row', None, 'col'), may hold values from -17 to 17, as said below
- panels: float32 [3, 1, 16, 512, 128], P(None, None, 'row', 'col'), may hold values from -0.25 to 0.25
- plan: int32 [3, 16], replicated, may hold values 0 or 1
Outputs:
- updated_tiles: float32 [1, 16, 1, 16, 1024, 1024], P(None, 'row', None, 'col')
Inputs may be any that keep to these rules, and one draw needn't show every extreme that they name: `matrix_tiles`: entries below the first subdiagonal of the matrix are zero.
All inputs are finite; a program needn't handle non-finite values.
Results may differ from a plain program's by a relative error of at most 0.0003.
Values sent between devices are 32-bit elements; how exact they have to be, the bound alone decides.
A program may use at most 64 MiB of HBM per device.

v0:
```python
import jax
import jax.numpy as jnp
from jax import lax
from jax.sharding import PartitionSpec as P

exact_mode = lax.Precision.HIGHEST


def broadcast(value, axis, source):
    kept = jnp.where(lax.axis_index(axis) == source, value, 0).astype(value.dtype)
    return lax.psum(kept, axis)


def passed_along(value, axis, steps):
    count = lax.axis_size(axis)
    pairs = [(source, (source + steps) % count) for source in range(count)]
    return lax.ppermute(value, axis, pairs)


def round_offsets(tile_size, window):
    return [0, tile_size - window // 2, window // 2]


def upper_inverse(upper_part):
    order_n = upper_part.shape[0]
    identity = jnp.eye(order_n, dtype=upper_part.dtype)
    scale = 1.0 / jnp.diag(upper_part)
    power = identity - upper_part * scale[:, None]
    result = identity + power
    span = 2
    while span < order_n:
        power = jnp.dot(power, power, precision=exact_mode)
        result = jnp.dot(result, identity + power, precision=exact_mode)
        span = span * 2
    return result * scale[None, :]


def window_factor(reflect):
    window, reflectors = reflect.shape
    gram_matrix = jnp.dot(reflect.T, reflect, precision=exact_mode)
    upper_part = jnp.triu(gram_matrix, 1) + jnp.diag(jnp.diag(gram_matrix) * 0.5)
    factor = upper_inverse(upper_part)
    product = jnp.dot(reflect, factor, precision=exact_mode)
    return jnp.eye(window, dtype=reflect.dtype) - jnp.dot(product, reflect.T, precision=exact_mode)


def live_mask(plan, tile_ids, offsets, window, tile_size):
    chosen = jnp.take(plan, tile_ids, axis=1) > 0
    inside = jnp.stack(
        [
            tile_ids < plan.shape[1] - 1 if offset + window > tile_size else tile_ids >= 0
            for offset in offsets
        ]
    )
    return jnp.logical_and(chosen, inside)


def on_device(matrix_tiles, panels, plan):
    rows_n = lax.axis_size("row")
    cols_n = lax.axis_size("col")
    row_at = lax.axis_index("row")
    col_at = lax.axis_index("col")
    row_tiles, _, col_tiles, _, tile_size, _ = matrix_tiles.shape
    rounds, _, _, _, reflectors = panels.shape
    matrix = matrix_tiles.reshape(row_tiles, col_tiles, tile_size, tile_size)
    gathered = lax.all_gather(panels, "col", axis=3, tiled=True)
    window = gathered.shape[3]
    half_width = window // 2
    panel_all = gathered.reshape(rounds, row_tiles, window, reflectors)
    offsets = round_offsets(tile_size, window)
    identity = jnp.eye(window, dtype=jnp.float32)
    factors = jax.vmap(window_factor)(panel_all.reshape(-1, window, reflectors)).reshape(
        rounds, row_tiles, window, window
    )
    left_ids = jnp.arange(row_tiles, dtype=jnp.int32) * rows_n + row_at
    left_live = live_mask(plan, left_ids, offsets, window, tile_size)
    left_q = jnp.where(left_live[:, :, None, None], factors, identity)
    right_ids = jnp.arange(col_tiles, dtype=jnp.int32) * cols_n + col_at
    source_row = col_at % rows_n
    picked = right_ids // rows_n
    received = broadcast(factors, "row", source_row)
    right_raw = jnp.take(received, picked, axis=1)
    right_live = live_mask(plan, right_ids, offsets, window, tile_size)
    right_q = jnp.where(right_live[:, :, None, None], right_raw, identity)
    last_row = row_at == rows_n - 1
    last_col = col_at == cols_n - 1
    for round_at in range(rounds):
        offset = offsets[round_at]
        left_now = left_q[round_at]
        right_now = right_q[round_at]
        if offset + window <= tile_size:
            window_rows = matrix[:, :, offset : offset + window, :]
            updated = jnp.einsum("ivw,ijvx->ijwx", left_now, window_rows, precision=exact_mode)
            matrix = matrix.at[:, :, offset : offset + window, :].set(updated)
            window_cols = matrix[:, :, :, offset : offset + window]
            updated = jnp.einsum("ijyv,jvw->ijyw", window_cols, right_now, precision=exact_mode)
            matrix = matrix.at[:, :, :, offset : offset + window].set(updated)
        else:
            from_below = passed_along(matrix[:, :, :half_width, :], "row", -1)
            from_below = jnp.where(last_row, jnp.roll(from_below, -1, axis=0), from_below)
            stacked = jnp.concatenate(
                [matrix[:, :, tile_size - half_width :, :], from_below], axis=2
            )
            updated = jnp.einsum("ivw,ijvx->ijwx", left_now, stacked, precision=exact_mode)
            going_back = updated[:, :, half_width:, :]
            going_back = jnp.where(last_row, jnp.roll(going_back, 1, axis=0), going_back)
            returned = passed_along(going_back, "row", 1)
            matrix = matrix.at[:, :, tile_size - half_width :, :].set(updated[:, :, :half_width, :])
            matrix = matrix.at[:, :, :half_width, :].set(returned)
            from_right = passed_along(matrix[:, :, :, :half_width], "col", -1)
            from_right = jnp.where(last_col, jnp.roll(from_right, -1, axis=1), from_right)
            stacked = jnp.concatenate(
                [matrix[:, :, :, tile_size - half_width :], from_right], axis=3
            )
            updated = jnp.einsum("ijyv,jvw->ijyw", stacked, right_now, precision=exact_mode)
            going_back = updated[:, :, :, half_width:]
            going_back = jnp.where(last_col, jnp.roll(going_back, 1, axis=1), going_back)
            returned = passed_along(going_back, "col", 1)
            matrix = matrix.at[:, :, :, tile_size - half_width :].set(updated[:, :, :, :half_width])
            matrix = matrix.at[:, :, :, :half_width].set(returned)
    return matrix.reshape(row_tiles, 1, col_tiles, 1, tile_size, tile_size)


def solution(mesh):
    placed = (P(None, "row", None, "col", None, None), P(None, None, "row", "col", None), P())
    return jax.shard_map(
        on_device,
        mesh=mesh,
        in_specs=placed,
        out_specs=P(None, "row", None, "col", None, None),
        check_vma=False,
    )
```

profile of v0, /device:TPU:39, one launch (start us, length us, event | category | flops | bytes accessed | tf_op | source)
XLA Modules:
  0.0 421.5 jit_solution(6370427126374975800)
XLA Ops:
  6.5 4.8 %copy.29 = f32[1,1,1,1,1024,1024]{5,4,3,2,1,0:T(8,128)} copy(f32[1,1,1,1,1024,1024]{5,4,3,2,1,0:T(8,128)} %param.21) | data formatting | bytes 8388608
  11.4 1.2 fusion.15
  12.6 45.0 %all_gather.3 = f32[3,1,1,512,128]{4,3,0,2,1:T(8,128)S(1)} all-gather(f32[3,1,1,32,128]{4,3,0,2,1:T(8,128)S(1)} %bitcast.123), channel_id=1, replica_groups=mesh['row'=16,'col'=16] {'col'}, dimensions={3}, use_global_device_ids=true | all-gather | bytes 835584 | tf_op jit(solution)/shard_map/all_gather | solution.py:66
  57.6 1.4 fusion.20
  59.0 4.6 %copy.6 = f32[3,128,128]{0,2,1:T(8,128)} copy(f32[3,128,128]{2,1,0:T(8,128)S(1)} %fusion.20) | data formatting | bytes 393216 | tf_op jit(solution)/shard_map/vmap()/dot_general | solution.py:40
  63.6 1.8 gather_fusion
  65.6 5.1 %copy.8 = f32[3,128,128]{0,2,1:T(8,128)} copy(f32[3,128,128]{2,1,0:T(8,128)S(1)} %select_add_fusion) | data formatting | bytes 393216 | tf_op jit(solution)/shard_map/vmap()/add | solution.py:41
  70.7 1.8 gather_fusion.1
  72.6 0.4 fusion.33
  73.0 0.4 fusion.30
  74.1 0.3 fusion.28
  74.8 0.3 fusion.26
  76.4 0.4 convolution_multiply_fusion
  76.8 0.8 fusion.18
  77.8 5.7 %select_bitcast_fusion = (f32[3,1,512,512]{3,2,0,1:T(8,128)}, f32[3,512,512]{2,1,0:T(8,128)S(1)}) fusion(f32[512,512]{1,0:T(8,128)S(1)} %copy-done.2, pred[]{:T(512)S(6)} %eq.46, pred[3]{0:T(512)(128)(4,1)S(1)} %get-tuple-element.114, f32[3,128,512]{1,2,0:T(8,128)S(1)} %fusion.18, f32[3,1,1,512,128]{4,3,0,2,1:T(8,128)} %copy-done.1), kind=kOutput, calls=%fused_computation.3 | convolution fusion | flops 1210318848 | bytes 8912900 | tf_op jit(solution)/shard_map/vmap()/dot_general | solution.py:44
  83.5 5.1 %fusion.3 = f32[512,1024]{1,0:T(8,128)S(1)} fusion(f32[1,1,1024,1024]{3,2,1,0:T(8,128)} %bitcast, f32[3,512,512]{2,1,0:T(8,128)S(1)} %get-tuple-element.120), kind=kOutput, calls=%fused_computation.12 | convolution fusion | flops 3221225472 | bytes 5242880 | tf_op jit(solution)/shard_map/ivw,ijvx->ijwx/dot_general | solution.py:93
  88.6 1.5 bitcast_dynamic-update-slice_fusion
  90.1 126.7 %all-reduce.2.cloned.1.call-done = f32[3,1,512,512]{3,2,0,1:T(8,128)} async-done(((f32[3,1,512,512]{3,2,0,1:T(8,128)}), f32[3,1,512,512]{3,2,0,1:T(8,128)}) %all-reduce.2.cloned.1.call-update) | async-done | bytes 3145744 | tf_op jit(solution)/shard_map/psum | solution.py:11
  216.8 2.8 select_select_fusion
  219.6 1.6 copy-done
  221.3 10.0 %fusion.12 = f32[1,1,1024,512]{2,3,0,1:T(8,128)} fusion(f32[1,1,1024,1024]{3,2,1,0:T(8,128)} %bitcast_dynamic-update-slice_fusion, f32[3,1,512,512]{3,2,0,1:T(8,128)S(1)} %select_select_fusion), kind=kOutput, calls=%fused_computation.24 | convolution fusion | flops 3221225472 | bytes 5242880 | tf_op jit(solution)/shard_map/ijyv,jvw->ijyw/dot_general | solution.py:96
  231.3 2.9 copy.11
  234.2 3.1 constant_dynamic-update-slice_fusion.6
  237.3 1.7 fusion.54
  239.0 16.3 %collective-permute-done = f32[1,1,256,1024]{3,2,1,0:T(8,128)S(1)} collective-permute-done((f32[1,1,256,1024]{3,2,1,0:T(8,128)S(1)}, f32[1,1,256,1024]{3,2,1,0:T(8,128)S(1)}, u32[]{:S(2)}, u32[]{:S(2)}) %collective-permute-start) | collective-permute-done | bytes 1048608 | tf_op jit(solution)/shard_map/ppermute | solution.py:17
  255.3 3.5 fusion.11
  258.9 1.5 fusion.56
  260.5 2.6 copy.12
  263.1 2.3 constant_dynamic-update-slice_fusion.5
  265.4 7.2 %collective-permute-done.1 = f32[1,1,256,1024]{2,3,1,0:T(8,128)} collective-permute-done((f32[1,1,256,1024]{2,3,1,0:T(8,128)}, f32[1,1,256,1024]{2,3,1,0:T(8,128)}, u32[]{:S(2)}, u32[]{:S(2)}) %collective-permute-start.1) | collective-permute-done | bytes 1048608 | tf_op jit(solution)/shard_map/ppermute | solution.py:17
  272.6 2.5 copy.13
  275.1 2.3 constant_dynamic-update-slice_fusion.4
  277.4 1.7 fusion.53
  279.1 5.2 %collective-permute-start.2 = (f32[1,1,1024,256]{3,2,1,0:T(8,128)S(1)}, f32[1,1,1024,256]{3,2,1,0:T(8,128)S(1)}, u32[]{:S(2)}, u32[]{:S(2)}) collective-permute-start(f32[1,1,1024,256]{3,2,1,0:T(8,128)S(1)} %get-tuple-element.116), channel_id=1, source_target_pairs={{0,15},{1,0},{2,1},{3,2},{4,3},{5,4},{6,5},{7,6},{8,7},{9,8},{10,9... | collective-permute-start | bytes 3145736 | tf_op jit(solution)/shard_map/ppermute | solution.py:17
  284.3 41.2 %collective-permute-done.2 = f32[1,1,1024,256]{3,2,1,0:T(8,128)S(1)} collective-permute-done((f32[1,1,1024,256]{3,2,1,0:T(8,128)S(1)}, f32[1,1,1024,256]{3,2,1,0:T(8,128)S(1)}, u32[]{:S(2)}, u32[]{:S(2)}) %collective-permute-start.2) | collective-permute-done | bytes 1048608 | tf_op jit(solution)/shard_map/ppermute | solution.py:17
  325.5 8.0 %fusion.10 = f32[1,1,1024,512]{2,3,0,1:T(8,128)S(1)} fusion(f32[1,1,1024,256]{3,2,1,0:T(8,128)S(1)} %collective-permute-done.2, f32[1,1,1024,256]{3,2,1,0:T(8,128)S(1)} %get-tuple-element.115, f32[3,1,512,512]{3,2,0,1:T(8,128)} %copy-done), kind=kOutput, calls=%fused_computation.22 | convolution fusion | flops 3221749760 | bytes 5242880 | tf_op jit(solution)/shard_map/ijyv,jvw->ijyw/dot_general | solution.py:115
  333.4 1.5 fusion.55
  335.2 2.6 copy.14
  337.7 2.3 constant_dynamic-update-slice_fusion.3
  340.0 46.3 %collective-permute-done.3 = f32[1,1,1024,256]{2,3,0,1:T(8,128)} collective-permute-done((f32[1,1,1024,256]{2,3,0,1:T(8,128)}, f32[1,1,1024,256]{2,3,0,1:T(8,128)}, u32[]{:S(2)}, u32[]{:S(2)}) %collective-permute-start.3) | collective-permute-done | bytes 1048608 | tf_op jit(solution)/shard_map/ppermute | solution.py:17
  386.3 2.5 copy.15
  388.8 2.3 constant_dynamic-update-slice_fusion.2
  391.1 6.4 %fusion.13 = f32[1,1,512,1024]{2,3,1,0:T(8,128)} fusion(f32[1,1,1024,1024]{3,2,1,0:T(8,128)} %constant_dynamic-update-slice_fusion.2, f32[3,512,512]{2,1,0:T(8,128)S(1)} %get-tuple-element.120), kind=kOutput, calls=%fused_computation.25 | convolution fusion | flops 3221225472 | bytes 5242880 | tf_op jit(solution)/shard_map/ivw,ijvx->ijwx/dot_general | solution.py:93
  397.5 1.9 copy.16
  399.4 1.5 constant_dynamic-update-slice_fusion.1
  400.8 10.0 %fusion.14 = f32[1,1,1,1,1024,512]{4,5,3,2,1,0:T(8,128)} fusion(f32[1,1,1024,1024]{3,2,1,0:T(8,128)} %constant_dynamic-update-slice_fusion.1, f32[3,1,512,512]{3,2,0,1:T(8,128)} %copy-done), kind=kOutput, calls=%fused_computation.26 | convolution fusion | flops 3221225472 | bytes 5242880 | tf_op jit(solution)/shard_map/ijyv,jvw->ijyw/dot_general | solution.py:96
  410.8 1.9 copy.17
  412.7 1.5 constant_dynamic-update-slice_fusion
  (30 shorter events, 3.3 us)
Async XLA Ops:
  6.5 6.0 %copy-start.3 = (f32[3,1,1,32,128]{4,3,2,1,0:T(8,128)S(1)}, f32[3,1,1,32,128]{4,3,2,1,0:T(8,128)}, u32[]{:S(2)}) copy-start(f32[3,1,1,32,128]{4,3,2,1,0:T(8,128)} %param.22) | copy-start | bytes 147460
  6.5 210.3 %all-reduce.2.cloned.1.call-start = ((), (), s32[]{:S(2)}) async-start(), calls=%async_computation | async-start | bytes 6291456 | tf_op jit(solution)/shard_map/psum | solution.py:11
  57.6 19.2 %copy-start.1 = (f32[3,1,1,512,128]{4,3,0,2,1:T(8,128)}, f32[3,1,1,512,128]{4,3,0,2,1:T(8,128)S(1)}, u32[]{:S(2)}) copy-start(f32[3,1,1,512,128]{4,3,0,2,1:T(8,128)S(1)} %all_gather.3) | copy-start | bytes 2359300
  74.4 3.2 copy-start.4
  74.4 3.4 copy-start.2
  219.6 1.6 copy-start
  238.9 16.4 %collective-permute-start = (f32[1,1,256,1024]{3,2,1,0:T(8,128)S(1)}, f32[1,1,256,1024]{3,2,1,0:T(8,128)S(1)}, u32[]{:S(2)}, u32[]{:S(2)}) collective-permute-start(f32[1,1,256,1024]{3,2,1,0:T(8,128)S(1)} %get-tuple-element.118), channel_id=1, source_target_pairs={{0,240},{16,0},{32,16},{48,32},{64,48},{80,64},{96,80},{112,96},{1... | collective-permute-start | bytes 3145736 | tf_op jit(solution)/shard_map/ppermute | solution.py:17
  260.3 12.3 %collective-permute-start.1 = (f32[1,1,256,1024]{2,3,1,0:T(8,128)}, f32[1,1,256,1024]{2,3,1,0:T(8,128)}, u32[]{:S(2)}, u32[]{:S(2)}) collective-permute-start(f32[1,1,256,1024]{2,3,1,0:T(8,128)} %get-tuple-element.123), channel_id=1, source_target_pairs={{0,16},{16,32},{32,48},{48,64},{64,80},{80,96},{96,112},{112,128},... | collective-permute-start | bytes 3145736 | tf_op jit(solution)/shard_map/ppermute | solution.py:17
  279.1 46.4 %collective-permute-start.2 = (f32[1,1,1024,256]{3,2,1,0:T(8,128)S(1)}, f32[1,1,1024,256]{3,2,1,0:T(8,128)S(1)}, u32[]{:S(2)}, u32[]{:S(2)}) collective-permute-start(f32[1,1,1024,256]{3,2,1,0:T(8,128)S(1)} %get-tuple-element.116), channel_id=1, source_target_pairs={{0,15},{1,0},{2,1},{3,2},{4,3},{5,4},{6,5},{7,6},{8,7},{9,8},{10,9... | collective-permute-start | bytes 3145736 | tf_op jit(solution)/shard_map/ppermute | solution.py:17
  334.9 51.4 %collective-permute-start.3 = (f32[1,1,1024,256]{2,3,0,1:T(8,128)}, f32[1,1,1024,256]{2,3,0,1:T(8,128)}, u32[]{:S(2)}, u32[]{:S(2)}) collective-permute-start(f32[1,1,1024,256]{2,3,0,1:T(8,128)} %get-tuple-element.121), channel_id=1, source_target_pairs={{0,1},{1,2},{2,3},{3,4},{4,5},{5,6},{6,7},{7,8},{8,9},{9,10},{10,1... | collective-permute-start | bytes 3145736 | tf_op jit(solution)/shard_map/ppermute | solution.py:17
Sparse Core Ops, SparseCore 0:
  83.6 133.1 all-reduce.1
where the time goes:
time: 425 us; the launch traced here: 422 us
  waiting for transfers between devices  238 us (56%)
  local copies, waits for them, and re-layouts  59.7 us (14%)
  matrix products  54.8 us (13%)
  blocking collectives  45 us (11%)
  between operations  14.2 us (3%)
  starting transfers between devices  5.72 us (1%)
  other arithmetic  4.4 us (1%)
    psum x1, waiting for transfers between devices, broadcast(): return lax.psum(kept, axis)  127 us
    ppermute x4, waiting for transfers between devices, passed_along(): return lax.ppermute(value, axis, pairs)  111 us
    all_gather x1, blocking collectives, on_device(): gathered = lax.all_gather(panels, 'col', axis=3, tiled=True)  45 us
    dot_general x2, matrix products, on_device(): jnp.einsum('ijyv,jvw->ijyw', window_cols, right_now, precision=exact_mode)  20 us
    dot_general x2, matrix products, on_device(): jnp.einsum('ivw,ijvx->ijwx', left_now, window_rows, precision=exact_mode)  11.5 us
  transfers between devices with their start and end apart: 5, of which 5 were waited for; matrix products, arithmetic and copies ran while one was open for 4% of the time, Pallas kernels for 0%

commit v1 on v0

--- a/solution.py
+++ b/solution.py
@@ -63,7 +63,9 @@
     row_tiles, _, col_tiles, _, tile_size, _ = matrix_tiles.shape
     rounds, _, _, _, reflectors = panels.shape
     matrix = matrix_tiles.reshape(row_tiles, col_tiles, tile_size, tile_size)
-    gathered = lax.all_gather(panels, "col", axis=3, tiled=True)
+    gathered = jnp.concatenate(
+        lax.all_to_all(jnp.stack([panels] * lax.axis_size("col")), "col", 0, 0), axis=3
+    )
     window = gathered.shape[3]
     half_width = window // 2
     panel_all = gathered.reshape(rounds, row_tiles, window, reflectors)

time: 425 us -> 411 us (0.967); the launches traced: 422 us -> 403 us
  blocking collectives: 45 us -> 0 us
  waiting for transfers between devices: 238 us -> 253 us
  starting transfers between devices: 5.72 us -> 16 us
    all_gather x1 -> x0, blocking collectives: 45 us -> none  [on_device(): gathered = lax.all_gather(panels, 'col', axis=3, tiled=True)]
    all_to_all x0 -> x1, waiting for transfers between devices: none -> 21.2 us  [on_device(): lax.all_to_all(jnp.stack([panels] * lax.axis_size('col')), 'col', 0, 0)]
    all_to_all x0 -> x1, starting transfers between devices: none -> 10 us  [on_device(): lax.all_to_all(jnp.stack([panels] * lax.axis_size('col')), 'col', 0, 0)]
    psum x1, waiting for transfers between devices: 127 us -> 121 us  [broadcast(): return lax.psum(kept, axis)]
  transfers between devices with their start and end apart: 5 -> 6, of which waited for: 5 -> 6; matrix products, arithmetic and copies ran while one was open for 4% -> 4% of each run, Pallas kernels for 0% -> 0%
where the time goes in v1:
time: 411 us; the launch traced here: 403 us
  waiting for transfers between devices  253 us (62%)
  local copies, waits for them, and re-layouts  62 us (15%)
  matrix products  54.3 us (13%)
  starting transfers between devices  16 us (4%)
  between operations  14 us (3%)
    psum x1, waiting for transfers between devices, broadcast(): return lax.psum(kept, axis)  121 us
    ppermute x4, waiting for transfers between devices, passed_along(): return lax.ppermute(value, axis, pairs)  111 us
    all_to_all x1, waiting for transfers between devices, on_device(): lax.all_to_all(jnp.stack([panels] * lax.axis_size('col')), 'col', 0, 0)  21.2 us
    dot_general x2, matrix products, on_device(): jnp.einsum('ijyv,jvw->ijyw', window_cols, right_now, precision=exact_mode)  19.9 us
    dot_general x2, matrix products, on_device(): jnp.einsum('ivw,ijvx->ijwx', left_now, window_rows, precision=exact_mode)  11.5 us
    all_to_all x1, starting transfers between devices, on_device(): lax.all_to_all(jnp.stack([panels] * lax.axis_size('col')), 'col', 0, 0)  10 us
    unnamed x11, local copies, waits for them, and re-layouts  8.26 us
  transfers between devices with their start and end apart: 6, of which 6 were waited for; matrix products, arithmetic and copies ran while one was open for 4% of the time, Pallas kernels for 0%

profile of v1, /device:TPU:39, one launch (start us, length us, event | category | flops | bytes accessed | tf_op | source)
XLA Modules:
  0.0 403.1 jit_solution(13967096942227960727)
XLA Ops:
  6.5 4.8 %copy.42 = f32[1,1,1,1,1024,1024]{5,4,3,2,1,0:T(8,128)} copy(f32[1,1,1,1,1024,1024]{5,4,3,2,1,0:T(8,128)} %param.21) | data formatting | bytes 8388608
  11.3 1.0 stack.17
  12.3 10.0 %all-to-all-start = ((f32[16,3,1,1,32,128]{5,4,1,3,2,0:T(8,128)}), f32[16,3,1,1,32,128]{5,4,1,3,2,0:T(8,128)S(1)}, u32[]{:S(2)}, u32[]{:S(2)}) async-start(f32[16,3,1,1,32,128]{5,4,1,3,2,0:T(8,128)} %stack.17), calls=%async_computation | async-start | bytes 1572864 | tf_op jit(solution)/shard_map/all_to_all | solution.py:67
  22.8 21.2 %all-to-all-done = f32[16,3,1,1,32,128]{5,4,1,3,2,0:T(8,128)S(1)} async-done(((f32[16,3,1,1,32,128]{5,4,1,3,2,0:T(8,128)}), f32[16,3,1,1,32,128]{5,4,1,3,2,0:T(8,128)S(1)}, u32[]{:S(2)}, u32[]{:S(2)}) %all-to-all-start) | async-done | bytes 786464 | tf_op jit(solution)/shard_map/all_to_all | solution.py:67
  44.1 1.4 fusion.51
  45.5 4.6 %copy.19 = f32[3,128,128]{0,2,1:T(8,128)} copy(f32[3,128,128]{2,1,0:T(8,128)S(1)} %fusion.51) | data formatting | bytes 393216 | tf_op jit(solution)/shard_map/vmap()/dot_general | solution.py:40
  50.1 1.8 gather_fusion
  52.1 4.6 %copy.21 = f32[3,128,128]{0,2,1:T(8,128)} copy(f32[3,128,128]{2,1,0:T(8,128)S(1)} %select_add_fusion) | data formatting | bytes 393216 | tf_op jit(solution)/shard_map/vmap()/add | solution.py:41
  56.7 1.8 gather_fusion.1
  58.6 0.4 fusion.27
  59.0 0.4 fusion.24
  62.4 0.4 convolution_multiply_fusion
  62.8 0.8 fusion.56
  63.6 5.2 %select_bitcast_fusion = (f32[3,1,512,512]{3,2,0,1:T(8,128)}, f32[3,512,512]{2,1,0:T(8,128)}) fusion(f32[512,512]{1,0:T(8,128)S(1)} %fusion.15, pred[]{:T(512)S(6)} %eq.46, pred[3]{0:T(512)(128)(4,1)S(1)} %get-tuple-element.114, f32[3,128,512]{1,2,0:T(8,128)S(1)} %fusion.56, f32[3,512,128]{2,1,0:T(8,128)S(1)} %bitcast.122), kind=kOutput, calls=%fused_computation.3 | convolution fusion | flops 1210318848 | bytes 8912900 | tf_op jit(solution)/shard_map/vmap()/dot_general | solution.py:44
  68.8 1.8 copy-done
  70.7 5.1 %fusion.3 = f32[512,1024]{1,0:T(8,128)S(1)} fusion(f32[1,1,1024,1024]{3,2,1,0:T(8,128)} %bitcast, f32[3,512,512]{2,1,0:T(8,128)S(1)} %copy-done), kind=kOutput, calls=%fused_computation.12 | convolution fusion | flops 3221225472 | bytes 5242880 | tf_op jit(solution)/shard_map/ivw,ijvx->ijwx/dot_general | solution.py:95
  75.8 1.5 bitcast_dynamic-update-slice_fusion
  77.2 121.3 %all-reduce.2.cloned.1.call-done = f32[3,1,512,512]{3,2,0,1:T(8,128)} async-done(((f32[3,1,512,512]{3,2,0,1:T(8,128)}), f32[3,1,512,512]{3,2,0,1:T(8,128)}) %all-reduce.2.cloned.1.call-update) | async-done | bytes 3145744 | tf_op jit(solution)/shard_map/psum | solution.py:11
  198.5 2.8 select_select_fusion
  201.3 1.6 copy-done.1
  202.9 9.9 %fusion.12 = f32[1,1,1024,512]{2,3,0,1:T(8,128)} fusion(f32[1,1,1024,1024]{3,2,1,0:T(8,128)} %bitcast_dynamic-update-slice_fusion, f32[3,1,512,512]{3,2,0,1:T(8,128)S(1)} %select_select_fusion), kind=kOutput, calls=%fused_computation.24 | convolution fusion | flops 3221225472 | bytes 5242880 | tf_op jit(solution)/shard_map/ijyv,jvw->ijyw/dot_general | solution.py:98
  212.8 2.9 copy.24
  215.7 3.1 constant_dynamic-update-slice_fusion.6
  218.8 1.7 fusion.48
  220.7 16.3 %collective-permute-done = f32[1,1,256,1024]{3,2,1,0:T(8,128)S(1)} collective-permute-done((f32[1,1,256,1024]{3,2,1,0:T(8,128)S(1)}, f32[1,1,256,1024]{3,2,1,0:T(8,128)S(1)}, u32[]{:S(2)}, u32[]{:S(2)}) %collective-permute-start) | collective-permute-done | bytes 1048608 | tf_op jit(solution)/shard_map/ppermute | solution.py:17
  237.0 3.5 fusion.11
  240.6 1.5 fusion.50
  242.0 2.5 copy.25
  244.6 2.3 constant_dynamic-update-slice_fusion.5
  246.9 7.2 %collective-permute-done.1 = f32[1,1,256,1024]{2,3,1,0:T(8,128)} collective-permute-done((f32[1,1,256,1024]{2,3,1,0:T(8,128)}, f32[1,1,256,1024]{2,3,1,0:T(8,128)}, u32[]{:S(2)}, u32[]{:S(2)}) %collective-permute-start.1) | collective-permute-done | bytes 1048608 | tf_op jit(solution)/shard_map/ppermute | solution.py:17
  254.1 2.5 copy.26
  256.6 2.3 constant_dynamic-update-slice_fusion.4
  258.9 1.7 fusion.47
  260.6 5.4 %collective-permute-start.2 = (f32[1,1,1024,256]{3,2,1,0:T(8,128)S(1)}, f32[1,1,1024,256]{3,2,1,0:T(8,128)S(1)}, u32[]{:S(2)}, u32[]{:S(2)}) collective-permute-start(f32[1,1,1024,256]{3,2,1,0:T(8,128)S(1)} %get-tuple-element.116), channel_id=1, source_target_pairs={{0,15},{1,0},{2,1},{3,2},{4,3},{5,4},{6,5},{7,6},{8,7},{9,8},{10,9... | collective-permute-start | bytes 3145736 | tf_op jit(solution)/shard_map/ppermute | solution.py:17
  266.0 41.2 %collective-permute-done.2 = f32[1,1,1024,256]{3,2,1,0:T(8,128)S(1)} collective-permute-done((f32[1,1,1024,256]{3,2,1,0:T(8,128)S(1)}, f32[1,1,1024,256]{3,2,1,0:T(8,128)S(1)}, u32[]{:S(2)}, u32[]{:S(2)}) %collective-permute-start.2) | collective-permute-done | bytes 1048608 | tf_op jit(solution)/shard_map/ppermute | solution.py:17
  307.2 8.0 %fusion.10 = f32[1,1,1024,512]{2,3,0,1:T(8,128)S(1)} fusion(f32[1,1,1024,256]{3,2,1,0:T(8,128)S(1)} %collective-permute-done.2, f32[1,1,1024,256]{3,2,1,0:T(8,128)S(1)} %get-tuple-element.115, f32[3,1,512,512]{3,2,0,1:T(8,128)} %copy-done.1), kind=kOutput, calls=%fused_computation.22 | convolution fusion | flops 3221749760 | bytes 5242880 | tf_op jit(solution)/shard_map/ijyv,jvw->ijyw/dot_general | solution.py:117
  315.1 1.5 fusion.49
  316.8 2.5 copy.27
  319.4 2.3 constant_dynamic-update-slice_fusion.3
  321.7 46.3 %collective-permute-done.3 = f32[1,1,1024,256]{2,3,0,1:T(8,128)} collective-permute-done((f32[1,1,1024,256]{2,3,0,1:T(8,128)}, f32[1,1,1024,256]{2,3,0,1:T(8,128)}, u32[]{:S(2)}, u32[]{:S(2)}) %collective-permute-start.3) | collective-permute-done | bytes 1048608 | tf_op jit(solution)/shard_map/ppermute | solution.py:17
  368.0 2.5 copy.28
  370.5 2.3 constant_dynamic-update-slice_fusion.2
  372.8 6.4 %fusion.13 = f32[1,1,512,1024]{2,3,1,0:T(8,128)} fusion(f32[1,1,1024,1024]{3,2,1,0:T(8,128)} %constant_dynamic-update-slice_fusion.2, f32[3,512,512]{2,1,0:T(8,128)S(1)} %copy-done), kind=kOutput, calls=%fused_computation.25 | convolution fusion | flops 3221225472 | bytes 5242880 | tf_op jit(solution)/shard_map/ivw,ijvx->ijwx/dot_general | solution.py:95
  379.2 1.9 copy.29
  381.1 1.5 constant_dynamic-update-slice_fusion.1
  382.6 10.0 %fusion.14 = f32[1,1,1,1,1024,512]{4,5,3,2,1,0:T(8,128)} fusion(f32[1,1,1024,1024]{3,2,1,0:T(8,128)} %constant_dynamic-update-slice_fusion.1, f32[3,1,512,512]{3,2,0,1:T(8,128)} %copy-done.1), kind=kOutput, calls=%fused_computation.26 | convolution fusion | flops 3221225472 | bytes 5242880 | tf_op jit(solution)/shard_map/ijyv,jvw->ijyw/dot_general | solution.py:98
  392.6 1.9 copy.30
  394.5 1.5 constant_dynamic-update-slice_fusion
  (33 shorter events, 4.2 us)
Async XLA Ops:
  6.5 4.8 %copy-start.3 = (f32[3,1,1,32,128]{4,3,2,1,0:T(8,128)S(1)}, f32[3,1,1,32,128]{4,3,2,1,0:T(8,128)}, u32[]{:S(2)}) copy-start(f32[3,1,1,32,128]{4,3,2,1,0:T(8,128)} %param.22) | copy-start | bytes 147460
  6.5 15.9 %copy-start.4 = (s32[3,16]{1,0:T(4,128)S(1)}, s32[3,16]{1,0:T(4,128)}, u32[]{:S(2)}) copy-start(s32[3,16]{1,0:T(4,128)} %param.23) | copy-start | bytes 580
  12.3 31.7 %all-to-all-start = ((f32[16,3,1,1,32,128]{5,4,1,3,2,0:T(8,128)}), f32[16,3,1,1,32,128]{5,4,1,3,2,0:T(8,128)S(1)}, u32[]{:S(2)}, u32[]{:S(2)}) async-start(f32[16,3,1,1,32,128]{5,4,1,3,2,0:T(8,128)} %stack.17), calls=%async_computation | async-start | bytes 1572864 | tf_op jit(solution)/shard_map/all_to_all | solution.py:67
  22.3 176.1 %all-reduce.2.cloned.1.call-start = ((), (), s32[]{:S(2)}) async-start(), calls=%async_computation.1 | async-start | bytes 6291456 | tf_op jit(solution)/shard_map/psum | solution.py:11
  22.8 40.7 %copy-start.2 = (f32[512,512]{1,0:T(8,128)}, f32[512,512]{1,0:T(8,128)S(1)}, u32[]{:S(2)}) copy-start(f32[512,512]{1,0:T(8,128)S(1)} %fusion.15) | copy-start | bytes 3145732
  68.8 1.9 copy-start
  201.3 1.6 copy-start.1
  220.5 16.6 %collective-permute-start = (f32[1,1,256,1024]{3,2,1,0:T(8,128)S(1)}, f32[1,1,256,1024]{3,2,1,0:T(8,128)S(1)}, u32[]{:S(2)}, u32[]{:S(2)}) collective-permute-start(f32[1,1,256,1024]{3,2,1,0:T(8,128)S(1)} %get-tuple-element.118), channel_id=1, source_target_pairs={{0,240},{16,0},{32,16},{48,32},{64,48},{80,64},{96,80},{112,96},{1... | collective-permute-start | bytes 3145736 | tf_op jit(solution)/shard_map/ppermute | solution.py:17
  242.0 12.1 %collective-permute-start.1 = (f32[1,1,256,1024]{2,3,1,0:T(8,128)}, f32[1,1,256,1024]{2,3,1,0:T(8,128)}, u32[]{:S(2)}, u32[]{:S(2)}) collective-permute-start(f32[1,1,256,1024]{2,3,1,0:T(8,128)} %get-tuple-element.123), channel_id=1, source_target_pairs={{0,16},{16,32},{32,48},{48,64},{64,80},{80,96},{96,112},{112,128},... | collective-permute-start | bytes 3145736 | tf_op jit(solution)/shard_map/ppermute | solution.py:17
  260.6 46.6 %collective-permute-start.2 = (f32[1,1,1024,256]{3,2,1,0:T(8,128)S(1)}, f32[1,1,1024,256]{3,2,1,0:T(8,128)S(1)}, u32[]{:S(2)}, u32[]{:S(2)}) collective-permute-start(f32[1,1,1024,256]{3,2,1,0:T(8,128)S(1)} %get-tuple-element.116), channel_id=1, source_target_pairs={{0,15},{1,0},{2,1},{3,2},{4,3},{5,4},{6,5},{7,6},{8,7},{9,8},{10,9... | collective-permute-start | bytes 3145736 | tf_op jit(solution)/shard_map/ppermute | solution.py:17
  316.6 51.4 %collective-permute-start.3 = (f32[1,1,1024,256]{2,3,0,1:T(8,128)}, f32[1,1,1024,256]{2,3,0,1:T(8,128)}, u32[]{:S(2)}, u32[]{:S(2)}) collective-permute-start(f32[1,1,1024,256]{2,3,0,1:T(8,128)} %get-tuple-element.121), channel_id=1, source_target_pairs={{0,1},{1,2},{2,3},{3,4},{4,5},{5,6},{6,7},{7,8},{8,9},{9,10},{10,1... | collective-permute-start | bytes 3145736 | tf_op jit(solution)/shard_map/ppermute | solution.py:17
Sparse Core Ops, SparseCore 0:
  68.9 129.5 all-reduce.1
